TPU v7x, 32 devices: a whole 2x2x4 slice. The times are simulated.
32 devices in a mesh: sect: 2 (over core), tok: 2 (over x), vocab: 8 (over z, y).
Axes of the slice: x: 2, y: 2, z: 4, core: 2. Of those that a mesh axis runs over, the one named last changes fastest.
Arguments:
- teacher_hidden: bfloat16 [512, 8192], P('tok', 'sect'), may hold values from -6 to 6
- teacher_head: bfloat16 [8192, 4096], P('sect', 'vocab'), may hold values from -0.19921875 to 0.19921875
- student_hidden: bfloat16 [512, 3072], P('tok', 'sect'), may hold values from -6 to 6
- student_head: bfloat16 [3072, 4096], P('sect', 'vocab'), may hold values from -0.328125 to 0.328125
- live_counts: int32 [2], P('tok'), may hold values from 1 to 256, 384 in all
Outputs:
- loss: float32 [], replicated
- head_grad: bfloat16 [3072, 4096], P(('sect', 'tok'), 'vocab')
- hidden_grad: bfloat16 [512, 3072], P(('tok', 'vocab'), 'sect')
Inputs may be any that keep to these rules, and one draw needn't show every extreme that they name: Shard k of the tokens has its first live_counts[k] token slots live and the rest empty.
All inputs are finite; a program needn't handle non-finite values.
Results may differ from a plain program's by a relative error of at most 0.0049.
Values may be sent and summed in bfloat16 or wider, within the bound.
A program may use at most 64 MiB of HBM per device.

v0:
```python
import jax
import jax.numpy as jnp
from jax import lax
from jax.sharding import PartitionSpec as P


def softened(teacher_logits, student_logits):
    teacher = teacher_logits * 0.5
    student = student_logits * 0.5
    teacher_exp = jnp.exp(teacher)
    student_exp = jnp.exp(student)
    partial_sums = (
        jnp.sum(teacher_exp, axis=1),
        jnp.sum(student_exp, axis=1),
        jnp.sum(teacher_exp * (teacher - student), axis=1),
    )
    return (teacher_exp, student_exp, partial_sums)


def finish(teacher_exp, student_exp, totals, live_rows, live_total, vocab_entries):
    teacher_sum, student_sum, cross = totals
    divergence = cross / teacher_sum - jnp.log(teacher_sum) + jnp.log(student_sum)
    numerator = jnp.sum(live_rows * divergence)
    row_scale = live_rows * (32.0 * vocab_entries * 0.5 / live_total)
    logit_grad = (
        row_scale[:, None]
        * (student_exp / student_sum[:, None] - teacher_exp / teacher_sum[:, None])
    ).astype(jnp.bfloat16)
    return (logit_grad, numerator)


def body(teacher_hidden, teacher_head, student_hidden, student_head, live_counts):
    token_rows = teacher_hidden.shape[0]
    vocab_entries = student_head.shape[1] * lax.axis_size("vocab")
    live_total = lax.psum(jnp.sum(live_counts.astype(jnp.float32)), "tok")
    live_rows = (jnp.arange(token_rows, dtype=jnp.int32) < live_counts[0]).astype(jnp.float32)
    teacher_part = jnp.dot(teacher_hidden, teacher_head, preferred_element_type=jnp.float32)
    student_part = jnp.dot(student_hidden, student_head, preferred_element_type=jnp.float32)
    teacher_logits, student_logits = lax.psum((teacher_part, student_part), "sect")
    teacher_exp, student_exp, partial_sums = softened(teacher_logits, student_logits)
    totals = lax.psum((partial_sums[0], partial_sums[1], partial_sums[2]), "vocab")
    logit_grad, numerator = finish(
        teacher_exp, student_exp, totals, live_rows, live_total, vocab_entries
    )
    owned_features = lax.all_to_all(student_hidden, "tok", split_axis=1, concat_axis=0, tiled=True)
    head_sum = lax.dot_general(
        owned_features,
        lax.all_gather(logit_grad, "tok", axis=0, tiled=True),
        (((0,), (0,)), ((), ())),
        preferred_element_type=jnp.float32,
    )
    head_grad = head_sum.astype(jnp.bfloat16)
    hidden_grad = lax.psum_scatter(
        lax.dot_general(
            logit_grad, student_head, (((1,), (1,)), ((), ())), preferred_element_type=jnp.float32
        ),
        "vocab",
        scatter_dimension=0,
        tiled=True,
    ).astype(jnp.bfloat16)
    loss = lax.psum(numerator, "tok") / live_total
    return (loss, head_grad, hidden_grad)


def solution(mesh):
    placed = (P("tok", "sect"), P("sect", "vocab"), P("tok", "sect"), P("sect", "vocab"), P("tok"))
    return jax.shard_map(
        body,
        mesh=mesh,
        in_specs=placed,
        out_specs=(P(), P(("sect", "tok"), "vocab"), P(("tok", "vocab"), "sect")),
        check_vma=False,
    )
```

profile of v0, /device:TPU:0, one launch (start us, length us, event | category | flops | bytes accessed | tf_op | source)
XLA Modules:
  0.0 144.1 jit_solution(9674600153131628786)
XLA Ops:
  7.2 0.0 copy-start
  7.2 0.0 copy-start.2
  7.2 0.0 all-reduce.5.cloned.1.call-start
  7.2 1.5 %copy-done = bf16[256,4096]{1,0:T(8,128)(2,1)S(1)} copy-done((bf16[256,4096]{1,0:T(8,128)(2,1)S(1)}, bf16[256,4096]{1,0:T(8,128)(2,1)}, u32[]{:S(2)}) %copy-start) | copy-done | bytes 2097176
  8.8 0.0 copy-start.1
  8.8 4.3 %fusion.3 = f32[256,512]{1,0:T(8,128)} fusion(bf16[256,4096]{1,0:T(8,128)(2,1)S(1)} %copy-done, bf16[4096,512]{1,0:T(8,128)(2,1)} %param.6), kind=kOutput, calls=%fused_computation.10 | convolution fusion | flops 1073741824 | bytes 6815744 | tf_op jit(solution)/shard_map/dot_general | solution.py:37
  13.1 0.0 copy-done.2
  13.1 0.0 copy-done.1
  13.1 1.4 fusion.4
  14.5 0.0 all-reduce.5.cloned.1.call-update
  14.5 0.0 reduce-scatter.2.cloned.1.call-start
  15.2 21.8 %all-reduce.5.cloned.1.call-done = (f32[256,512]{1,0:T(8,128)}, f32[256,512]{1,0:T(8,128)}) async-done(((f32[256,512]{1,0:T(8,128)}, f32[256,512]{1,0:T(8,128)}), (f32[256,512]{1,0:T(8,128)}, f32[256,512]{1,0:T(8,128)})) %all-reduce.5.cloned.1.call-update) | async-done | bytes 1048592 | tf_op jit(solution)/shard_map/psum | solution.py:39
  37.0 1.5 %multiply_reduce_fusion = (f32[256]{0:T(256)S(1)}, f32[256]{0:T(256)S(1)}, f32[256]{0:T(256)S(1)}) fusion(f32[256,512]{1,0:T(8,128)} %get-tuple-element.20, f32[256,512]{1,0:T(8,128)} %get-tuple-element.21), kind=kLoop, calls=%fused_computation.3 | loop fusion | flops 916736 | bytes 1051648 | tf_op jit(solution)/shard_map/reduce_sum | solution.py:15
  38.6 21.6 %all-reduce = (f32[256]{0:T(256)S(1)}, f32[256]{0:T(256)S(1)}, f32[256]{0:T(256)S(1)}) all-reduce(f32[256]{0:T(256)S(1)} %get-tuple-element.13, f32[256]{0:T(256)S(1)} %get-tuple-element.14, f32[256]{0:T(256)S(1)} %get-tuple-element.12), channel_id=1, replica_groups=mesh['sect'=2,'tok'=2,'vocab'=8] {'vocab'}, use_global_device_ids=true, to_apply=%region_7.0 | all-reduce | flops 768 | bytes 6144 | tf_op jit(solution)/shard_map/psum | solution.py:41
  60.2 0.6 select_reduce_fusion
  60.8 6.2 %all-reduce.1 = (f32[]{:T(128)}, f32[]{:T(128)}) all-reduce(f32[]{:T(128)} %select_reduce_fusion, f32[]{:T(128)} %bitcast.1), channel_id=1, replica_groups=mesh['sect'=2,'tok'=2,'vocab'=8] {'tok'}, use_global_device_ids=true, to_apply=%region_9.0 | all-reduce | flops 2 | bytes 16 | tf_op jit(solution)/shard_map/psum | solution.py:61
  67.7 1.4 multiply_convert_fusion
  69.1 3.2 %fusion.5 = f32[256,1536]{1,0:T(8,128)} fusion(bf16[256,512]{1,0:T(8,128)(2,1)S(1)} %multiply_convert_fusion, bf16[1536,512]{1,0:T(8,128)(2,1)} %param.8), kind=kOutput, calls=%fused_computation.12 | convolution fusion | flops 402653184 | bytes 3407872 | tf_op jit(solution)/shard_map/dot_general | solution.py:54
  72.3 0.0 reduce-scatter.2.cloned.1.call-update
  72.3 1.2 copy.10
  73.4 11.5 %all_to_all.19 = bf16[256,2,768]{0,2,1:T(8,128)(2,1)S(1)} all-to-all(bf16[256,2,768]{0,2,1:T(8,128)(2,1)} %bitcast.18), channel_id=1, replica_groups=mesh['sect'=2,'tok'=2,'vocab'=8] {'tok'}, dimensions={1} | all-to-all | bytes 1572864 | tf_op jit(solution)/shard_map/all_to_all | solution.py:45
  84.9 1.2 copy.11
  87.4 7.0 %all_gather.3 = bf16[512,512]{1,0:T(8,128)(2,1)S(1)} all-gather(bf16[256,512]{1,0:T(8,128)(2,1)S(1)} %multiply_convert_fusion), channel_id=1, replica_groups=mesh['sect'=2,'tok'=2,'vocab'=8] {'tok'}, dimensions={0}, use_global_device_ids=true | all-gather | bytes 786432 | tf_op jit(solution)/shard_map/all_gather | solution.py:48
  94.5 1.7 %fusion = bf16[768,512]{0,1:T(8,128)(2,1)S(1)} fusion(bf16[512,512]{1,0:T(8,128)(2,1)S(1)} %all_gather.3, bf16[512,768]{1,0:T(8,128)(2,1)} %bitcast.19), kind=kOutput, calls=%fused_computation.1 | convolution fusion | flops 403046400 | bytes 2097152 | tf_op jit(solution)/shard_map/dot_general | solution.py:46
  96.2 1.2 copy.12
  97.4 37.2 %reduce-scatter.2.cloned.1.call-done = f32[32,1536]{1,0:T(8,128)} async-done(((f32[256,1536]{1,0:T(8,128)}), f32[32,1536]{1,0:T(8,128)}) %reduce-scatter.2.cloned.1.call-update) | async-done | bytes 196624 | tf_op jit(solution)/shard_map/reduce_scatter | solution.py:53
  134.5 1.6 %convert_element_type.20 = bf16[32,1536]{1,0:T(8,128)(2,1)} convert(f32[32,1536]{1,0:T(8,128)} %reduce-scatter.2.cloned.1.call-done) | non-fusion elementwise | flops 49152 | bytes 294912 | tf_op jit(solution)/shard_map/convert_element_type | solution.py:60
  (1 shorter events, 0.0 us)
Async XLA Ops:
  7.2 1.6 %copy-start = (bf16[256,4096]{1,0:T(8,128)(2,1)S(1)}, bf16[256,4096]{1,0:T(8,128)(2,1)}, u32[]{:S(2)}) copy-start(bf16[256,4096]{1,0:T(8,128)(2,1)} %param.5) | copy-start | bytes 6291460
  7.2 5.9 %copy-start.2 = (bf16[256,1536]{1,0:T(8,128)(2,1)S(1)}, bf16[256,1536]{1,0:T(8,128)(2,1)}, u32[]{:S(2)}) copy-start(bf16[256,1536]{1,0:T(8,128)(2,1)} %param.7) | copy-start | bytes 2359300
  7.2 29.9 %all-reduce.5.cloned.1.call-start = ((), (), s32[]{:S(2)}) async-start(), calls=%async_computation.3 | async-start | bytes 2097152 | tf_op jit(solution)/shard_map/psum | solution.py:39
  8.8 4.4 %copy-start.1 = (bf16[1536,512]{1,0:T(8,128)(2,1)S(1)}, bf16[1536,512]{1,0:T(8,128)(2,1)}, u32[]{:S(2)}) copy-start(bf16[1536,512]{1,0:T(8,128)(2,1)} %param.8) | copy-start | bytes 4718596
  14.5 120.0 %reduce-scatter.2.cloned.1.call-start = ((), (), s32[]{:S(2)}) async-start(), calls=%async_computation.2 | async-start | bytes 1769472 | tf_op jit(solution)/shard_map/reduce_scatter | solution.py:53
Sparse Core Ops, SparseCore 0:
  14.7 22.3 all-reduce.4
  72.4 62.0 reduce-scatter.1
where the time goes:
time: 145 us; the launch traced here: 144 us
  waiting for transfers between devices  59 us (41%)
  blocking collectives  46.3 us (32%)
  between operations  17.9 us (12%)
  matrix products  10.6 us (7%)
  other arithmetic  5.12 us (4%)
  local copies, waits for them, and re-layouts  5.01 us (3%)
    reduce_scatter x1, waiting for transfers between devices, body(): lax.psum_scatter(lax.dot_general(logit_grad, student_head, (((1,), (1,)),...  37.2 us
    psum x1, waiting for transfers between devices, body(): lax.psum((teacher_part, student_part), 'sect')  21.8 us
    psum x1, blocking collectives, body(): lax.psum((partial_sums[0], partial_sums[1], partial_sums[2]), 'vocab')  21.6 us
    all_to_all x1, blocking collectives, body(): lax.all_to_all(student_hidden, 'tok', split_axis=1, concat_axis=0, tiled=...  11.5 us
    all_gather x1, blocking collectives, body(): lax.all_gather(logit_grad, 'tok', axis=0, tiled=True)  7.05 us
    psum x1, blocking collectives, body(): loss = lax.psum(numerator, 'tok') / live_total  6.16 us
    dot_general x1, matrix products, body(): jnp.dot(teacher_hidden, teacher_head, preferred_element_type=jnp.float32)  4.34 us
    unnamed x8, local copies, waits for them, and re-layouts  3.86 us
  transfers between devices with their start and end apart: 2, of which 2 were waited for; matrix products, arithmetic and copies ran while one was open for 4% of the time, Pallas kernels for 0%

commit v1 on v0

--- a/solution.py
+++ b/solution.py
@@ -2,6 +2,7 @@
 import jax.numpy as jnp
 from jax import lax
 from jax.sharding import PartitionSpec as P
+from jax.lax import all_gather
 
 
 def softened(teacher_logits, student_logits):
@@ -58,7 +59,12 @@
         scatter_dimension=0,
         tiled=True,
     ).astype(jnp.bfloat16)
-    loss = lax.psum(numerator, "tok") / live_total
+
+    def attach_sectors(xs, comm_axis):
+        opened = jnp.sum(all_gather(xs, comm_axis), axis=0)
+        return opened
+
+    loss = attach_sectors(numerator, "tok") / live_total
     return (loss, head_grad, hidden_grad)
 
 

time: 145 us -> 146 us (level)
  local copies, waits for them, and re-layouts: 5.01 us -> 7.06 us
    psum x1 -> x0, blocking collectives: 6.16 us -> none  [body(): loss = lax.psum(numerator, 'tok') / live_total]
    unnamed x0 -> x1, blocking collectives: none -> 6.13 us
    unnamed x8 -> x13, local copies, waits for them, and re-layouts: 3.86 us -> 5.9 us
where the time goes in v1:
time: 146 us; the launch traced here: 145 us
  waiting for transfers between devices  57.7 us (40%)
  blocking collectives  46.3 us (32%)
  between operations  17.9 us (12%)
  matrix products  10.6 us (7%)
  local copies, waits for them, and re-layouts  7.06 us (5%)
  other arithmetic  5.72 us (4%)
    reduce_scatter x1, waiting for transfers between devices, body(): lax.psum_scatter(lax.dot_general(logit_grad, student_head, (((1,), (1,)),...  36.5 us
    psum x1, blocking collectives, body(): lax.psum((partial_sums[0], partial_sums[1], partial_sums[2]), 'vocab')  21.6 us
    psum x1, waiting for transfers between devices, body(): lax.psum((teacher_part, student_part), 'sect')  21.1 us
    all_to_all x1, blocking collectives, body(): lax.all_to_all(student_hidden, 'tok', split_axis=1, concat_axis=0, tiled=...  11.5 us
    all_gather x1, blocking collectives, body(): lax.all_gather(logit_grad, 'tok', axis=0, tiled=True)  7.05 us
    unnamed x1, blocking collectives  6.13 us
    unnamed x13, local copies, waits for them, and re-layouts  5.9 us
    dot_general x1, matrix products, body(): jnp.dot(teacher_hidden, teacher_head, preferred_element_type=jnp.float32)  4.34 us
  transfers between devices with their start and end apart: 2, of which 2 were waited for; matrix products, arithmetic and copies ran while one was open for 4% of the time, Pallas kernels for 0%

profile of v1, /device:TPU:0, one launch (start us, length us, event | category | flops | bytes accessed | tf_op | source)
XLA Modules:
  0.0 145.4 jit_solution(12762695057096685967)
XLA Ops:
  7.2 0.0 copy-start
  7.2 0.0 copy-start.2
  7.2 0.0 all-reduce.6.cloned.1.call-start
  7.2 1.5 %copy-done = bf16[256,4096]{1,0:T(8,128)(2,1)S(1)} copy-done((bf16[256,4096]{1,0:T(8,128)(2,1)S(1)}, bf16[256,4096]{1,0:T(8,128)(2,1)}, u32[]{:S(2)}) %copy-start) | copy-done | bytes 2097176
  8.8 0.0 copy-start.1
  8.8 4.3 %fusion.3 = f32[256,512]{1,0:T(8,128)} fusion(bf16[256,4096]{1,0:T(8,128)(2,1)S(1)} %copy-done, bf16[4096,512]{1,0:T(8,128)(2,1)} %param.6), kind=kOutput, calls=%fused_computation.10 | convolution fusion | flops 1073741824 | bytes 6815744 | tf_op jit(solution)/shard_map/dot_general | solution.py:38
  13.1 0.0 copy-done.2
  13.1 0.0 copy-done.1
  13.1 0.0 copy-start.3
  13.1 1.4 fusion.4
  14.5 0.0 all-reduce.6.cloned.1.call-update
  14.5 0.0 reduce-scatter.2.cloned.1.call-start
  15.2 0.0 copy-done.3
  15.2 0.7 dynamic-slice
  15.9 21.1 %all-reduce.6.cloned.1.call-done = (f32[256,512]{1,0:T(8,128)}, f32[256,512]{1,0:T(8,128)}) async-done(((f32[256,512]{1,0:T(8,128)}, f32[256,512]{1,0:T(8,128)}), (f32[256,512]{1,0:T(8,128)}, f32[256,512]{1,0:T(8,128)})) %all-reduce.6.cloned.1.call-update) | async-done | bytes 1048592 | tf_op jit(solution)/shard_map/psum | solution.py:40
  37.1 1.5 %multiply_reduce_fusion = (f32[256]{0:T(256)S(1)}, f32[256]{0:T(256)S(1)}, f32[256]{0:T(256)S(1)}) fusion(f32[256,512]{1,0:T(8,128)} %get-tuple-element.20, f32[256,512]{1,0:T(8,128)} %get-tuple-element.21), kind=kLoop, calls=%fused_computation.3 | loop fusion | flops 916736 | bytes 1051648 | tf_op jit(solution)/shard_map/reduce_sum | solution.py:16
  38.6 21.6 %all-reduce.1 = (f32[256]{0:T(256)S(1)}, f32[256]{0:T(256)S(1)}, f32[256]{0:T(256)S(1)}) all-reduce(f32[256]{0:T(256)S(1)} %get-tuple-element.13, f32[256]{0:T(256)S(1)} %get-tuple-element.14, f32[256]{0:T(256)S(1)} %get-tuple-element.12), channel_id=1, replica_groups=mesh['sect'=2,'tok'=2,'vocab'=8] {'vocab'}, use_global_device_ids=true, to_apply=%region_7.0 | all-reduce | flops 768 | bytes 6144 | tf_op jit(solution)/shard_map/psum | solution.py:42
  60.2 0.6 select_reduce_fusion
  60.8 1.4 dynamic-update-slice
  62.2 6.1 %all-reduce.2 = (f32[2]{0:T(128)S(1)}, f32[]{:T(128)}) all-reduce(f32[2]{0:T(128)S(1)} %dynamic-update-slice, f32[]{:T(128)} %bitcast.3), channel_id=1, replica_groups=mesh['sect'=2,'tok'=2,'vocab'=8] {'tok'}, use_global_device_ids=true, to_apply=%add | all-reduce | flops 3 | bytes 24
  69.0 1.4 multiply_convert_fusion
  70.5 3.2 %fusion.5 = f32[256,1536]{1,0:T(8,128)} fusion(bf16[256,512]{1,0:T(8,128)(2,1)S(1)} %multiply_convert_fusion, bf16[1536,512]{1,0:T(8,128)(2,1)} %param.8), kind=kOutput, calls=%fused_computation.12 | convolution fusion | flops 402653184 | bytes 3407872 | tf_op jit(solution)/shard_map/dot_general | solution.py:55
  73.6 0.0 reduce-scatter.2.cloned.1.call-update
  73.7 1.2 copy.10
  74.8 11.5 %all_to_all.19 = bf16[256,2,768]{0,2,1:T(8,128)(2,1)S(1)} all-to-all(bf16[256,2,768]{0,2,1:T(8,128)(2,1)} %bitcast.20), channel_id=1, replica_groups=mesh['sect'=2,'tok'=2,'vocab'=8] {'tok'}, dimensions={1} | all-to-all | bytes 1572864 | tf_op jit(solution)/shard_map/all_to_all | solution.py:46
  86.3 1.2 copy.11
  87.5 0.6 reduce_sum.55
  89.4 7.0 %all_gather.11 = bf16[512,512]{1,0:T(8,128)(2,1)S(1)} all-gather(bf16[256,512]{1,0:T(8,128)(2,1)S(1)} %multiply_convert_fusion), channel_id=1, replica_groups=mesh['sect'=2,'tok'=2,'vocab'=8] {'tok'}, dimensions={0}, use_global_device_ids=true | all-gather | bytes 786432 | tf_op jit(solution)/shard_map/all_gather | solution.py:49
  96.5 1.7 %fusion = bf16[768,512]{0,1:T(8,128)(2,1)S(1)} fusion(bf16[512,512]{1,0:T(8,128)(2,1)S(1)} %all_gather.11, bf16[512,768]{1,0:T(8,128)(2,1)} %bitcast.21), kind=kOutput, calls=%fused_computation.1 | convolution fusion | flops 403046400 | bytes 2097152 | tf_op jit(solution)/shard_map/dot_general | solution.py:47
  98.2 1.2 copy.12
  99.3 36.5 %reduce-scatter.2.cloned.1.call-done = f32[32,1536]{1,0:T(8,128)} async-done(((f32[256,1536]{1,0:T(8,128)}), f32[32,1536]{1,0:T(8,128)}) %reduce-scatter.2.cloned.1.call-update) | async-done | bytes 196624 | tf_op jit(solution)/shard_map/reduce_scatter | solution.py:54
  135.9 1.6 %convert_element_type.20 = bf16[32,1536]{1,0:T(8,128)(2,1)} convert(f32[32,1536]{1,0:T(8,128)} %reduce-scatter.2.cloned.1.call-done) | non-fusion elementwise | flops 49152 | bytes 294912 | tf_op jit(solution)/shard_map/convert_element_type | solution.py:61
  (2 shorter events, 0.0 us)
Async XLA Ops:
  7.2 1.6 %copy-start = (bf16[256,4096]{1,0:T(8,128)(2,1)S(1)}, bf16[256,4096]{1,0:T(8,128)(2,1)}, u32[]{:S(2)}) copy-start(bf16[256,4096]{1,0:T(8,128)(2,1)} %param.5) | copy-start | bytes 6291460
  7.2 5.9 %copy-start.2 = (bf16[256,1536]{1,0:T(8,128)(2,1)S(1)}, bf16[256,1536]{1,0:T(8,128)(2,1)}, u32[]{:S(2)}) copy-start(bf16[256,1536]{1,0:T(8,128)(2,1)} %param.7) | copy-start | bytes 2359300
  7.2 29.9 %all-reduce.6.cloned.1.call-start = ((), (), s32[]{:S(2)}) async-start(), calls=%async_computation.3 | async-start | bytes 2097152 | tf_op jit(solution)/shard_map/psum | solution.py:40
  8.8 4.4 %copy-start.1 = (bf16[1536,512]{1,0:T(8,128)(2,1)S(1)}, bf16[1536,512]{1,0:T(8,128)(2,1)}, u32[]{:S(2)}) copy-start(bf16[1536,512]{1,0:T(8,128)(2,1)} %param.8) | copy-start | bytes 4718596
  13.1 2.1 %copy-start.3 = (u32[32]{0:T(128)S(1)}, u32[32]{0:T(128)}, u32[]{:S(2)}) copy-start(u32[32]{0:T(128)} %constant.11) | copy-start | bytes 388
  14.5 121.3 %reduce-scatter.2.cloned.1.call-start = ((), (), s32[]{:S(2)}) async-start(), calls=%async_computation.2 | async-start | bytes 1769472 | tf_op jit(solution)/shard_map/reduce_scatter | solution.py:54
Sparse Core Ops, SparseCore 0:
  14.7 22.3 all-reduce.5
  73.8 62.0 reduce-scatter.1
